TPU v7x, 32 devices: a whole 2x2x4 slice. The times are simulated.
32 devices in a mesh: seq: 8 (over y, x, core), head: 4 (over z).
Axes of the slice: x: 2, y: 2, z: 4, core: 2. Of those that a mesh axis runs over, the one named last changes fastest.
Arguments:
- tokens: bfloat16 [32768, 512], P(('seq', 'head')), may hold values from -8.4 to 8.4
- cotangent: bfloat16 [32768, 512], P(('seq', 'head')), may hold values from -6 to 6
- w_qkv: bfloat16 [512, 1536], P(('seq', 'head')), may hold values from -0.25 to 0.25
- w_out: bfloat16 [512, 512], P(('seq', 'head')), may hold values from -0.5 to 0.5
- w_up: bfloat16 [512, 2048], P(None, ('seq', 'head')), may hold values from -0.25 to 0.25
- w_down: bfloat16 [2048, 512], P(('seq', 'head')), may hold values from -0.1875 to 0.1875
- gain_one: bfloat16 [512], P(('seq', 'head')), may hold values from 0.099609375 to 1.8984375
- shift_one: bfloat16 [512], P(('seq', 'head')), may hold values from -1.5 to 1.5
- gain_two: bfloat16 [512], P(('seq', 'head')), may hold values from 0.099609375 to 1.8984375
- shift_two: bfloat16 [512], P(('seq', 'head')), may hold values from -1.5 to 1.5
- span_doc: int32 [128], replicated, may hold values from 0 to 15, never falling along the last dimension, each value on 1 to 16 neighbouring positions
Outputs:
- out_tokens: bfloat16 [32768, 512], P(('seq', 'head'))
- d_tokens: float32 [32768, 512], P(('seq', 'head'))
- d_w_qkv: float32 [512, 1536], P(('seq', 'head'))
- d_w_out: float32 [512, 512], P(('seq', 'head'))
- d_w_up: float32 [512, 2048], P(None, ('seq', 'head'))
- d_w_down: float32 [2048, 512], P(('seq', 'head'))
- d_gain_one: float32 [512], P(('seq', 'head'))
- d_shift_one: float32 [512], P(('seq', 'head'))
- d_gain_two: float32 [512], P(('seq', 'head'))
- d_shift_two: float32 [512], P(('seq', 'head'))
Inputs may be any that keep to these rules, and one draw needn't show every extreme that they name: span_doc[j] is the document of continuation span j; the numbers never fall along j, every continuation holds 1 to 16 spans, and one holds exactly 16.
All inputs are finite; a program needn't handle non-finite values.
Results may differ from a plain program's by a relative error of at most 0.012.
Values may be sent and summed in bfloat16 or wider, within the bound.
A program may use at most 128 MiB of HBM per device.

v0:
```python
import math
import jax
import jax.numpy as jnp
from jax import lax
from jax.sharding import PartitionSpec as P

H = 8
HD = 64
S = 128
QB = 512
MOST = 16
PSPANS = 128
epsilon = 1e-05
masked_score = -1e30


def layer_norm(values, gain, shift):
    row_mean = jnp.mean(values, axis=-1, keepdims=True)
    centred = values - row_mean
    variance = jnp.mean(centred * centred, axis=-1, keepdims=True)
    return centred * lax.rsqrt(variance + epsilon) * gain + shift


def gelu_tanh(values):
    return jax.nn.gelu(values, approximate=True)


def window_rows(first_span, sum_keys_all, sum_vals_all, docs_all):
    spans_blk = QB // S
    window = MOST + spans_blk
    win_start = jnp.maximum(first_span - MOST, 0)
    win_keys = lax.dynamic_slice_in_dim(sum_keys_all, win_start, window, 0)
    win_vals = lax.dynamic_slice_in_dim(sum_vals_all, win_start, window, 0)
    win_docs = lax.dynamic_slice_in_dim(docs_all, win_start, window, 0)
    sum_keys = jnp.concatenate([sum_keys_all[:PSPANS], win_keys], axis=0)
    sum_vals = jnp.concatenate([sum_vals_all[:PSPANS], win_vals], axis=0)
    sum_index = jnp.concatenate(
        [jnp.arange(PSPANS, dtype=jnp.int32), win_start + jnp.arange(window, dtype=jnp.int32)]
    )
    row_docs = jnp.concatenate([jnp.full((PSPANS,), -2, jnp.int32), win_docs])
    prompt_row = jnp.arange(PSPANS + window) < PSPANS
    query_span = first_span + jnp.arange(spans_blk, dtype=jnp.int32)
    query_doc = lax.dynamic_slice_in_dim(docs_all, first_span, spans_blk, 0)
    earlier = sum_index[None, :] < query_span[:, None]
    same_doc = (sum_index[None, :] >= PSPANS) & (row_docs[None, :] == query_doc[:, None])
    allowed = (earlier & (prompt_row[None, :] | same_doc))[:, None, :]
    return (sum_keys, sum_vals, allowed, win_start)


def block_logits(q_spans, k_blk, sum_keys, allowed):
    score_scale = 1.0 / math.sqrt(HD)
    direct = (
        jnp.einsum("nihe,njhe->hnij", q_spans, k_blk, preferred_element_type=jnp.float32)
        * score_scale
    )
    causal = jnp.arange(S)[:, None] >= jnp.arange(S)[None, :]
    direct = jnp.where(causal, direct, masked_score)
    summary = (
        jnp.einsum("nihe,the->hnit", q_spans, sum_keys, preferred_element_type=jnp.float32)
        * score_scale
    )
    summary = jnp.where(allowed, summary, masked_score)
    return (direct, summary)


def shards(
    tokens,
    cotangent,
    w_qkv,
    w_out,
    w_up,
    w_down,
    gain_one,
    shift_one,
    gain_two,
    shift_two,
    span_doc,
):
    seq_count = lax.axis_size("seq")
    head_count = lax.axis_size("head")
    tok_rows = tokens.shape[0]
    spans_blk = QB // S
    score_scale = 1.0 / math.sqrt(HD)
    grad_scale = 1.0 / math.sqrt(tok_rows * seq_count * head_count)
    docs_all = jnp.concatenate([jnp.full((PSPANS,), -1, jnp.int32), span_doc])
    qkv_mat, out_mat, up_mat, down_mat, gone_full, sone_full, gtwo_full, stwo_full = (
        lax.all_gather(w_qkv, ("seq", "head"), axis=0, tiled=True),
        lax.all_gather(w_out, ("seq", "head"), axis=0, tiled=True),
        lax.all_gather(w_up, ("seq", "head"), axis=1, tiled=True),
        lax.all_gather(w_down, ("seq", "head"), axis=0, tiled=True),
        lax.all_gather(gain_one, ("seq", "head"), axis=0, tiled=True),
        lax.all_gather(shift_one, ("seq", "head"), axis=0, tiled=True),
        lax.all_gather(gain_two, ("seq", "head"), axis=0, tiled=True),
        lax.all_gather(shift_two, ("seq", "head"), axis=0, tiled=True),
    )
    gone_full = gone_full.astype(jnp.float32)
    sone_full = sone_full.astype(jnp.float32)
    gtwo_full = gtwo_full.astype(jnp.float32)
    stwo_full = stwo_full.astype(jnp.float32)
    x_rows = tokens.astype(jnp.float32)
    norm_one, back_one = jax.vjp(layer_norm, x_rows, gone_full, sone_full)
    act_one = norm_one.astype(jnp.bfloat16)
    qkv_rows = jnp.dot(act_one, qkv_mat, preferred_element_type=jnp.float32).astype(jnp.bfloat16)
    heads_dev = H // head_count
    tok_grp = tok_rows * head_count
    group_index = lax.axis_index("seq")
    qkv_local = lax.all_to_all(qkv_rows, "head", split_axis=1, concat_axis=0, tiled=True)
    spans_grp = tok_grp // S
    all_spans = spans_grp * seq_count
    block_count = tok_grp // QB
    grouped = qkv_local.reshape(tok_grp, heads_dev, 3, HD)
    pair_part = grouped[:, :, 1:].reshape(spans_grp, S, heads_dev * 2 * HD)
    span_kv = (jnp.sum(pair_part, axis=1, dtype=jnp.float32) / S).astype(jnp.bfloat16)
    all_kv = lax.all_gather(span_kv, "seq", axis=0, tiled=True)
    all_kv = all_kv.reshape(all_spans, heads_dev, 2, HD)
    sum_keys_all = all_kv[:, :, 0]
    sum_vals_all = all_kv[:, :, 1]
    block_ids = jnp.arange(block_count, dtype=jnp.int32)
    q_blocks = grouped[:, :, 0].reshape(block_count, spans_blk, S, heads_dev, HD)
    k_blocks = grouped[:, :, 1].reshape(block_count, spans_blk, S, heads_dev, HD)
    v_blocks = grouped[:, :, 2].reshape(block_count, spans_blk, S, heads_dev, HD)

    def forward_block(inputs):
        block_id, q_spans, k_blk, v_blk = inputs
        first_span = group_index * spans_grp + block_id * spans_blk
        sum_keys, sum_vals, allowed, win_start = window_rows(
            first_span, sum_keys_all, sum_vals_all, docs_all
        )
        direct, summary = block_logits(q_spans, k_blk, sum_keys, allowed)
        row_top = jnp.maximum(jnp.max(direct, axis=-1), jnp.max(summary, axis=-1))
        exp_dir = jnp.exp(direct - row_top[..., None])
        exp_sum = jnp.exp(summary - row_top[..., None])
        denominator = jnp.sum(exp_dir, axis=-1) + jnp.sum(exp_sum, axis=-1)
        low_dir = (exp_dir / denominator[..., None]).astype(jnp.bfloat16)
        lower_total_sum = (exp_sum / denominator[..., None]).astype(jnp.bfloat16)
        mixed_rows = jnp.einsum(
            "hnij,njhe->nihe", low_dir, v_blk, preferred_element_type=jnp.float32
        )
        mixed_rows = mixed_rows + jnp.einsum(
            "hnit,the->nihe", lower_total_sum, sum_vals, preferred_element_type=jnp.float32
        )
        return (
            mixed_rows.astype(jnp.bfloat16).reshape(QB, heads_dev * HD),
            row_top + jnp.log(denominator),
        )

    local_attention, log_totals = lax.map(forward_block, (block_ids, q_blocks, k_blocks, v_blocks))
    local_attention = local_attention.reshape(tok_grp, heads_dev * HD)
    attn_rows = lax.all_to_all(local_attention, "head", split_axis=0, concat_axis=1, tiled=True)
    resid = x_rows + jnp.dot(attn_rows, out_mat, preferred_element_type=jnp.float32)
    norm_two, back_two = jax.vjp(layer_norm, resid, gtwo_full, stwo_full)
    act_two = norm_two.astype(jnp.bfloat16)
    hidden = jnp.dot(act_two, up_mat, preferred_element_type=jnp.float32)
    acted, back_gelu = jax.vjp(gelu_tanh, hidden)
    acted_low = acted.astype(jnp.bfloat16)
    out_rows = resid + jnp.dot(acted_low, down_mat, preferred_element_type=jnp.float32)
    d_acted = jnp.dot(cotangent, down_mat.T, preferred_element_type=jnp.float32)
    d_hidden = back_gelu(d_acted)[0].astype(jnp.bfloat16)
    grad_down = jnp.dot(acted_low.T, cotangent, preferred_element_type=jnp.float32)
    grad_up = jnp.dot(act_two.T, d_hidden, preferred_element_type=jnp.float32)
    d_norm_two = jnp.dot(d_hidden, up_mat.T, preferred_element_type=jnp.float32)
    out_tokens = out_rows.astype(jnp.bfloat16)
    d_resid_norm, grad_gain_two, grad_shift_two = back_two(d_norm_two)
    d_resid = cotangent.astype(jnp.float32) + d_resid_norm
    d_branch = d_resid.astype(jnp.bfloat16)
    grad_out = jnp.dot(attn_rows.T, d_branch, preferred_element_type=jnp.float32)
    d_attn = jnp.dot(d_branch, out_mat.T, preferred_element_type=jnp.float32).astype(jnp.bfloat16)
    local_gradient = lax.all_to_all(d_attn, "head", split_axis=1, concat_axis=0, tiled=True)
    do_blocks = local_gradient.reshape(block_count, spans_blk, S, heads_dev, HD)

    def backward_block(sum_grads, inputs):
        block_id, q_spans, k_blk, v_blk, output_span_gradient, log_blk = inputs
        first_span = group_index * spans_grp + block_id * spans_blk
        sum_keys, sum_vals, allowed, win_start = window_rows(
            first_span, sum_keys_all, sum_vals_all, docs_all
        )
        direct, summary = block_logits(q_spans, k_blk, sum_keys, allowed)
        prob_dir = jnp.exp(direct - log_blk[..., None])
        prob_sum = jnp.exp(summary - log_blk[..., None])
        low_dir = prob_dir.astype(jnp.bfloat16)
        lower_total_sum = prob_sum.astype(jnp.bfloat16)
        grad_dir = jnp.einsum(
            "nihe,njhe->hnij", output_span_gradient, v_blk, preferred_element_type=jnp.float32
        )
        grad_sum = jnp.einsum(
            "nihe,the->hnit", output_span_gradient, sum_vals, preferred_element_type=jnp.float32
        )
        delta = jnp.sum(prob_dir * grad_dir, axis=-1) + jnp.sum(prob_sum * grad_sum, axis=-1)
        ds_dir = (prob_dir * (grad_dir - delta[..., None])).astype(jnp.bfloat16)
        ds_sum = (prob_sum * (grad_sum - delta[..., None])).astype(jnp.bfloat16)
        d_query = jnp.einsum("hnij,njhe->nihe", ds_dir, k_blk, preferred_element_type=jnp.float32)
        d_query = (
            d_query
            + jnp.einsum("hnit,the->nihe", ds_sum, sum_keys, preferred_element_type=jnp.float32)
        ) * score_scale
        d_key = (
            jnp.einsum("hnij,nihe->njhe", ds_dir, q_spans, preferred_element_type=jnp.float32)
            * score_scale
        )
        d_value = jnp.einsum(
            "hnij,nihe->njhe", low_dir, output_span_gradient, preferred_element_type=jnp.float32
        )
        summary_key_gradient = (
            jnp.einsum("kord,orkj->dkj", ds_sum, q_spans, preferred_element_type=jnp.float32)
            * score_scale
        )
        summary_value_gradient = jnp.einsum(
            "kord,orkj->dkj",
            lower_total_sum,
            output_span_gradient,
            preferred_element_type=jnp.float32,
        )
        paired_gradient = jnp.stack([summary_key_gradient, summary_value_gradient], axis=2)
        sum_grads = sum_grads.at[:PSPANS].add(paired_gradient[:PSPANS])
        current = lax.dynamic_slice_in_dim(sum_grads, win_start, MOST + spans_blk, 0)
        sum_grads = lax.dynamic_update_slice_in_dim(
            sum_grads, current + paired_gradient[PSPANS:], win_start, 0
        )
        return (sum_grads, (d_query, d_key, d_value))

    start_grads = jnp.zeros((all_spans, heads_dev, 2, HD), jnp.float32)
    sum_grads, (dq_blocks, dk_blocks, dv_blocks) = lax.scan(
        backward_block,
        start_grads,
        (block_ids, q_blocks, k_blocks, v_blocks, do_blocks, log_totals),
    )
    flat_grads = sum_grads.reshape(all_spans, heads_dev * 2 * HD)
    span_grads = lax.psum_scatter(
        flat_grads.astype(jnp.bfloat16), "seq", scatter_dimension=0, tiled=True
    ).astype(jnp.float32)
    span_grads = span_grads.reshape(spans_grp, 1, heads_dev, 2, HD) / S
    d_key_all = dk_blocks.reshape(spans_grp, S, heads_dev, HD) + span_grads[:, :, :, 0]
    d_val_all = dv_blocks.reshape(spans_grp, S, heads_dev, HD) + span_grads[:, :, :, 1]
    d_qkv_local = jnp.stack(
        [
            dq_blocks.reshape(tok_grp, heads_dev, HD),
            d_key_all.reshape(tok_grp, heads_dev, HD),
            d_val_all.reshape(tok_grp, heads_dev, HD),
        ],
        axis=2,
    )
    d_qkv_local = d_qkv_local.astype(jnp.bfloat16).reshape(tok_grp, heads_dev * 3 * HD)
    d_qkv_rows = lax.all_to_all(d_qkv_local, "head", split_axis=0, concat_axis=1, tiled=True)
    grad_qkv = jnp.dot(act_one.T, d_qkv_rows, preferred_element_type=jnp.float32)
    d_norm_one = jnp.dot(d_qkv_rows, qkv_mat.T, preferred_element_type=jnp.float32)
    d_x_norm, grad_gain_one, first_shift_gradient = back_one(d_norm_one)
    d_tokens = d_resid + d_x_norm
    (
        grad_qkv,
        grad_out,
        grad_up,
        grad_down,
        grad_gain_one,
        first_shift_gradient,
        grad_gain_two,
        grad_shift_two,
    ) = (
        lax.psum_scatter(grad_qkv, ("seq", "head"), scatter_dimension=0, tiled=True),
        lax.psum_scatter(grad_out, ("seq", "head"), scatter_dimension=0, tiled=True),
        lax.psum_scatter(grad_up, ("seq", "head"), scatter_dimension=1, tiled=True),
        lax.psum_scatter(grad_down, ("seq", "head"), scatter_dimension=0, tiled=True),
        lax.psum_scatter(grad_gain_one, ("seq", "head"), scatter_dimension=0, tiled=True),
        lax.psum_scatter(first_shift_gradient, ("seq", "head"), scatter_dimension=0, tiled=True),
        lax.psum_scatter(grad_gain_two, ("seq", "head"), scatter_dimension=0, tiled=True),
        lax.psum_scatter(grad_shift_two, ("seq", "head"), scatter_dimension=0, tiled=True),
    )
    return (
        out_tokens,
        d_tokens,
        grad_qkv * grad_scale,
        grad_out * grad_scale,
        grad_up * grad_scale,
        grad_down * grad_scale,
        grad_gain_one * grad_scale,
        first_shift_gradient * grad_scale,
        grad_gain_two * grad_scale,
        grad_shift_two * grad_scale,
    )


def solution(mesh):
    in_specs = (
        P(("seq", "head"), None),
        P(("seq", "head"), None),
        P(("seq", "head"), None),
        P(("seq", "head"), None),
        P(None, ("seq", "head")),
        P(("seq", "head"), None),
        P(("seq", "head")),
        P(("seq", "head")),
        P(("seq", "head")),
        P(("seq", "head")),
        P(),
    )
    out_specs = (
        P(("seq", "head"), None),
        P(("seq", "head"), None),
        P(("seq", "head"), None),
        P(("seq", "head"), None),
        P(None, ("seq", "head")),
        P(("seq", "head"), None),
        P(("seq", "head")),
        P(("seq", "head")),
        P(("seq", "head")),
        P(("seq", "head")),
    )
    return jax.shard_map(shards, mesh=mesh, in_specs=in_specs, out_specs=out_specs, check_vma=False)
```

profile of v0, /device:TPU:0, one launch (start us, length us, event | category | flops | bytes accessed | tf_op | source)
XLA Modules:
  0.0 1173.3 jit_solution(1539304039287238738)
XLA Ops:
  11.3 42.1 %all-reduce.12 = (bf16[512]{0:T(512)(128)(2,1)S(1)}, bf16[512]{0:T(512)(128)(2,1)S(1)}, bf16[512]{0:T(512)(128)(2,1)}, bf16[512]{0:T(512)(128)(2,1)}) all-reduce(bf16[512]{0:T(512)(128)(2,1)S(1)} %dynamic-update-slice.7, bf16[512]{0:T(512)(128)(2,1)S(1)} %dynamic-update-slice.6, ...), channel_id=1, replica_groups=mesh['seq'=8,'head'=4] {'seq','head'}, use_global_device_ids=true, to_apply=%add.4 | all-reduce | flops 2048 | bytes 8192
  56.0 12.7 %all-gather.4.cloned.1.call-done = bf16[512,1536]{1,0:T(8,128)(2,1)} async-done(((bf16[16,1536]{1,0:T(8,128)(2,1)}), bf16[512,1536]{1,0:T(8,128)(2,1)}) %all-gather.4.cloned.1.call-update) | async-done | bytes 1572880 | tf_op jit(solution)/shard_map/all_gather | solution.py:87
  68.7 5.1 convolution_convert_fusion
  73.8 4.6 copy.204
  78.4 4.8 all-to-all-start
  84.8 74.1 %all-to-all-done = bf16[1024,4,384]{0,2,1:T(8,128)(2,1)} async-done(((bf16[1024,4,384]{0,2,1:T(8,128)(2,1)}), bf16[1024,4,384]{0,2,1:T(8,128)(2,1)}, u32[]{:S(2)}, u32[]{:S(2)}) %all-to-all-start) | async-done | bytes 3145760 | tf_op jit(solution)/shard_map/all_to_all | solution.py:107
  158.9 6.0 copy.163
  164.9 6.1 reshape.339
  171.0 3.6 fusion.89
  174.6 2.4 slice_convert_fusion
  178.2 2.7 reshape_squeeze.9
  184.1 4.9 copy.232
  189.0 3.3 reduce_sum.178
  192.5 9.2 all_gather.30
  202.9 68.9 %while.33 = (s32[]{:T(128)}, bf16[8,512,128]{2,1,0:T(8,128)(2,1)}, f32[8,2,4,128]{3,2,1,0:T(4,128)}, bf16[8,4,128,2,64]{2,1,0,4,3:T(4,128)(2,1)}, bf16[8,4,128,2...) while((s32[]{:T(128)}, bf16[8,512,128]{2,1,0:T(8,128)(2,1)}, ...), condition=%wide.region_8.9_spmd, body=%wide.region_3.8_spmd.sunk | while | flops 74914296 | bytes 5989179 | solution.py:147
  271.9 4.4 all-to-all-start.1
  279.2 90.4 %all_gather.31 = bf16[512,512]{1,0:T(8,128)(2,1)} all-gather(bf16[16,512]{1,0:T(8,128)(2,1)S(1)} %copy-done.18), channel_id=1, replica_groups=mesh['seq'=8,'head'=4] {'seq','head'}, dimensions={0}, use_global_device_ids=true | all-gather | bytes 540672 | tf_op jit(solution)/shard_map/all_gather | solution.py:88
  374.6 7.6 fusion.83
  382.2 9.7 fusion.63
  391.9 3.6 fusion.92
  395.5 2.9 copy.173
  404.8 3.5 all-to-all-start.2
  408.6 20.8 %all-to-all-done.2 = bf16[1024,4,128]{0,2,1:T(8,128)(2,1)S(1)} async-done(((bf16[1024,4,128]{0,2,1:T(8,128)(2,1)}), bf16[1024,4,128]{0,2,1:T(8,128)(2,1)S(1)}, u32[]{:S(2)}, u32[]{:S(2)}) %all-to-all-start.2) | async-done | bytes 1048608 | tf_op jit(solution)/shard_map/all_to_all | solution.py:168
  433.5 120.3 %while.34 = (s32[]{:T(128)}, f32[256,2,2,64]{0,3,1,2:T(8,128)S(1)}, bf16[8,4,128,2,64]{2,4,3,1,0:T(8,128)(2,1)}, f32[8,4,128,2,64]{2,1,0,4,3:T(4,128)}, f32[8,4,...) while((s32[]{:T(128)}, f32[256,2,2,64]{0,3,1,2:T(8,128)S(1)}, ...), condition=%wide.region_16.17_spmd, body=%wide.region_13.16_spmd.sunk | while | flops 183960576 | bytes 14116731 | solution.py:222
  554.7 3.3 fusion.93
  558.1 9.1 fusion.84
  568.8 6.7 fusion.82
  575.5 3.1 reshape.343
  578.5 3.0 copy.179
  581.5 2.6 stack_reshape.6
  584.2 3.1 reshape.342
  590.7 2.7 add.315
  595.5 2.7 add.319
  598.2 4.1 add_convert_fusion
  604.7 6.2 convert_element_type.128
  610.9 4.6 copy.184
  615.5 4.8 all-to-all-start.3
  620.5 76.7 %all-to-all-done.3 = bf16[4,1024,384]{1,2,0:T(8,128)(2,1)} async-done(((bf16[4,1024,384]{1,2,0:T(8,128)(2,1)}), bf16[4,1024,384]{1,2,0:T(8,128)(2,1)}, u32[]{:S(2)}, u32[]{:S(2)}) %all-to-all-start.3) | async-done | bytes 3145760 | tf_op jit(solution)/shard_map/all_to_all | solution.py:243
  697.2 5.6 fusion.79
  702.8 8.4 add_convert_fusion.2
  711.2 2.4 copy.188
  713.6 45.2 %reduce-scatter.10.cloned.1.call-done = f32[16,512]{1,0:T(8,128)} async-done(((f32[512,512]{1,0:T(8,128)}), f32[16,512]{1,0:T(8,128)}) %reduce-scatter.10.cloned.1.call-update) | async-done | bytes 32784 | tf_op jit(solution)/shard_map/reduce_scatter | solution.py:259
  760.2 5.1 fusion.91
  772.0 2.9 copy.189
  774.9 40.1 %all-reduce.11 = (f32[512]{0:T(512)S(1)}, f32[512]{0:T(512)S(1)}, f32[512]{0:T(512)S(1)}, f32[512]{0:T(512)S(1)}) all-reduce(f32[512]{0:T(512)S(1)} %get-tuple-element.526, f32[512]{0:T(512)S(1)} %get-tuple-element.617, f32[512]{0:T(512)S(1)} %get-tuple-element.524, ...), channel_id=7, replica_groups=mesh['seq'=8,'head'=4] {'seq','head'}, use_global_device_ids=true, to_apply=%region_25.26.clone | all-reduce | flops 2048 | bytes 16384
  817.3 92.8 %reduce-scatter.14.cloned.1.call-done = f32[64,512]{1,0:T(8,128)} async-done(((f32[2048,512]{1,0:T(8,128)}), f32[64,512]{1,0:T(8,128)}) %reduce-scatter.14.cloned.1.call-update) | async-done | bytes 131088 | tf_op jit(solution)/shard_map/reduce_scatter | solution.py:261
  911.6 147.4 %reduce-scatter.12.cloned.1.call-done = f32[512,64]{0,1:T(8,128)} async-done(((f32[512,2048]{0,1:T(8,128)}), f32[512,64]{0,1:T(8,128)}) %reduce-scatter.12.cloned.1.call-update) | async-done | bytes 131088 | tf_op jit(solution)/shard_map/reduce_scatter | solution.py:260
  1060.6 104.2 %reduce-scatter.8.cloned.1.call-done = f32[16,1536]{1,0:T(8,128)} async-done(((f32[512,1536]{1,0:T(8,128)}), f32[16,1536]{1,0:T(8,128)}) %reduce-scatter.8.cloned.1.call-update) | async-done | bytes 98320 | tf_op jit(solution)/shard_map/reduce_scatter | solution.py:258
  (647 shorter events, 235.3 us)
Async XLA Ops:
  7.2 61.6 %all-gather.4.cloned.1.call-start = ((), (), s32[]{:S(2)}) async-start(), calls=%async_computation.9 | async-start | bytes 1622016 | tf_op jit(solution)/shard_map/all_gather | solution.py:87
  53.4 15.3 %copy-start.19 = (f32[512]{0:T(512)}, f32[512]{0:T(512)S(1)}, u32[]{:S(2)}) copy-start(f32[512]{0:T(512)S(1)} %convert_element_type.110) | copy-start | bytes 6148
  55.4 0.6 copy-start.16
  78.4 6.3 copy-start.26
  78.4 80.4 %all-to-all-start = ((bf16[1024,4,384]{0,2,1:T(8,128)(2,1)}), bf16[1024,4,384]{0,2,1:T(8,128)(2,1)}, u32[]{:S(2)}, u32[]{:S(2)}) async-start(bf16[1024,4,384]{0,2,1:T(8,128)(2,1)} %bitcast.293), calls=%async_computation | async-start | bytes 6291456 | tf_op jit(solution)/shard_map/all_to_all | solution.py:107
  83.2 291.0 %all-gather.6.cloned.1.call-start = ((), (), s32[]{:S(2)}) async-start(), calls=%async_computation.10 | async-start | bytes 2162688 | tf_op jit(solution)/shard_map/all_gather | solution.py:89
  84.0 298.2 %all-gather.8.cloned.1.call-start = ((), (), s32[]{:S(2)}) async-start(), calls=%async_computation.11 | async-start | bytes 2162688 | tf_op jit(solution)/shard_map/all_gather | solution.py:90
  171.0 3.6 copy-start.4
  178.2 2.7 copy-start.12
  271.8 4.4 copy-start.24
  271.9 7.3 copy-start.2
  271.9 7.3 copy-start.10
  271.9 4.4 copy-start.23
  271.9 4.5 copy-start.22
  271.9 7.3 copy-start.18
  271.9 97.6 %all-to-all-start.1 = ((bf16[4,1024,128]{2,1,0:T(8,128)(2,1)}), bf16[4,1024,128]{2,1,0:T(8,128)(2,1)}, u32[]{:S(2)}, u32[]{:S(2)}) async-start(bf16[4,1024,128]{2,1,0:T(8,128)(2,1)} %bitcast.297), calls=%async_computation.1 | async-start | bytes 2097152 | tf_op jit(solution)/shard_map/all_to_all | solution.py:149
  373.9 26.9 %copy-start = (f32[1024,512]{0,1:T(8,128)}, f32[1024,512]{0,1:T(8,128)S(1)}, u32[]{:S(2)}) copy-start(f32[1024,512]{0,1:T(8,128)S(1)} %get-tuple-element.616) | copy-start | bytes 6291460
  373.9 0.6 copy-start.21
  382.1 9.7 copy-start.27
  391.8 3.7 copy-start.29
  398.4 2.4 copy-start.5
  400.8 1.2 copy-start.8
  401.4 1.3 copy-start.6
  402.0 1.1 copy-start.13
  403.1 1.7 copy-start.14
  404.8 24.6 %all-to-all-start.2 = ((bf16[1024,4,128]{0,2,1:T(8,128)(2,1)}), bf16[1024,4,128]{0,2,1:T(8,128)(2,1)S(1)}, u32[]{:S(2)}, u32[]{:S(2)}) async-start(bf16[1024,4,128]{0,2,1:T(8,128)(2,1)} %bitcast.43), calls=%async_computation.2 | async-start | bytes 2097152 | tf_op jit(solution)/shard_map/all_to_all | solution.py:168
  408.4 179.6 %reduce-scatter.16.cloned.1.call-start = ((), (), s32[]{:S(2)}) async-start(), calls=%async_computation.16 | async-start | bytes 147456
  429.4 4.1 copy-start.3
  429.4 4.1 copy-start.25
  554.6 3.5 copy-start.15
  554.6 204.2 %reduce-scatter.10.cloned.1.call-start = ((), (), s32[]{:S(2)}) async-start(), calls=%async_computation.13 | async-start | bytes 1081344 | tf_op jit(solution)/shard_map/reduce_scatter | solution.py:259
  558.0 352.0 %reduce-scatter.14.cloned.1.call-start = ((), (), s32[]{:S(2)}) async-start(), calls=%async_computation.15 | async-start | bytes 4325376 | tf_op jit(solution)/shard_map/reduce_scatter | solution.py:261
  567.2 1.6 copy-start.1
  567.2 491.8 %reduce-scatter.12.cloned.1.call-start = ((), (), s32[]{:S(2)}) async-start(), calls=%async_computation.14 | async-start | bytes 4325376 | tf_op jit(solution)/shard_map/reduce_scatter | solution.py:260
  598.2 4.1 copy-start.11
  615.5 81.8 %copy-start.20 = (f32[512]{0:T(512)S(1)}, f32[512]{0:T(512)}, u32[]{:S(2)}) copy-start(f32[512]{0:T(512)} %copy-done.19) | copy-start | bytes 6148
  615.5 81.8 %all-to-all-start.3 = ((bf16[4,1024,384]{1,2,0:T(8,128)(2,1)}), bf16[4,1024,384]{1,2,0:T(8,128)(2,1)}, u32[]{:S(2)}, u32[]{:S(2)}) async-start(bf16[4,1024,384]{1,2,0:T(8,128)(2,1)} %copy.184), calls=%async_computation.3 | async-start | bytes 6291456 | tf_op jit(solution)/shard_map/all_to_all | solution.py:243
  620.3 544.5 %reduce-scatter.8.cloned.1.call-start = ((), (), s32[]{:S(2)}) async-start(), calls=%async_computation.12 | async-start | bytes 3244032 | tf_op jit(solution)/shard_map/reduce_scatter | solution.py:258
  711.2 49.0 %copy-start.28 = (bf16[512,1536]{1,0:T(8,128)(2,1)S(1)}, bf16[512,1536]{1,0:T(8,128)(2,1)}, u32[]{:S(2)}) copy-start(bf16[512,1536]{1,0:T(8,128)(2,1)} %all-gather.4.cloned.1.call-done) | copy-start | bytes 4718596
  767.2 0.7 copy-start.17
  767.9 1.6 copy-start.7
  767.9 1.9 copy-start.9
Sparse Core Ops, SparseCore 0:
  10.9 57.8 all-gather.3
  87.0 90.1 all-gather.5
  180.1 55.4 all-gather.7
  554.7 33.1 reduce-scatter.15
  590.1 168.6 reduce-scatter.9
  760.9 149.0 reduce-scatter.13
  912.3 146.6 reduce-scatter.11
  1064.4 100.2 reduce-scatter.7
where the time goes:
time: 1180 us; the launch traced here: 1170 us
  waiting for transfers between devices  576 us (49%)
  local copies, waits for them, and re-layouts  213 us (18%)
  blocking collectives  182 us (15%)
  matrix products  118 us (10%)
  other arithmetic  37.9 us (3%)
  starting transfers between devices  19.1 us (2%)
  between operations  14.8 us (1%)
  loops' own time  12 us (1%)
    reduce_scatter x1, waiting for transfers between devices, shards(): lax.psum_scatter(grad_up, ('seq', 'head'), scatter_dimension=1, tiled=True)  147 us
    reduce_scatter x1, waiting for transfers between devices, shards(): lax.psum_scatter(grad_qkv, ('seq', 'head'), scatter_dimension=0, tiled=True)  104 us
    reduce_scatter x1, waiting for transfers between devices, shards(): lax.psum_scatter(grad_down, ('seq', 'head'), scatter_dimension=0, tiled=T...  92.8 us
    all_gather x1, blocking collectives, shards(): lax.all_gather(w_out, ('seq', 'head'), axis=0, tiled=True)  90.4 us
    unnamed x2, blocking collectives  82.1 us
    all_to_all x1, waiting for transfers between devices, shards(): lax.all_to_all(d_qkv_local, 'head', split_axis=0, concat_axis=1, tiled=True)  76.7 us
    all_to_all x1, waiting for transfers between devices, shards(): lax.all_to_all(qkv_rows, 'head', split_axis=1, concat_axis=0, tiled=True)  74.1 us
    reduce_scatter x1, waiting for transfers between devices, shards(): lax.psum_scatter(grad_out, ('seq', 'head'), scatter_dimension=0, tiled=True)  45.2 us
  transfers between devices with their start and end apart: 12, of which 9 were waited for; matrix products, arithmetic and copies ran while one was open for 18% of the time, Pallas kernels for 0%

commit v1 on v0

--- a/solution.py
+++ b/solution.py
@@ -104,7 +104,19 @@
     heads_dev = H // head_count
     tok_grp = tok_rows * head_count
     group_index = lax.axis_index("seq")
-    qkv_local = lax.all_to_all(qkv_rows, "head", split_axis=1, concat_axis=0, tiled=True)
+    ways, here = (lax.axis_size("head"), lax.axis_index("head"))
+    width = qkv_rows.shape[1] // ways
+    shape = list(qkv_rows.shape)
+    shape[1] = width
+    height = shape[0]
+    shape[0] = height * ways
+    full = jnp.zeros(shape, qkv_rows.dtype)
+    for mask in range(ways):
+        part = lax.dynamic_slice_in_dim(qkv_rows, (here ^ mask) * width, width, axis=1)
+        if mask:
+            part = lax.ppermute(part, "head", [(d, d ^ mask) for d in range(ways)])
+        full = lax.dynamic_update_slice_in_dim(full, part, (here ^ mask) * height, axis=0)
+    qkv_local = full
     spans_grp = tok_grp // S
     all_spans = spans_grp * seq_count
     block_count = tok_grp // QB

time: 1180 us -> 1170 us (level)
  waiting for transfers between devices: 576 us -> 546 us
  starting transfers between devices: 19.1 us -> 38.5 us
    all_to_all x1 -> x0, waiting for transfers between devices: 74.1 us -> none  [shards(): lax.all_to_all(qkv_rows, 'head', split_axis=1, concat_axis=0, tiled=True)]
    ppermute x0 -> x3, waiting for transfers between devices: none -> 44.7 us  [shards(): part = lax.ppermute(part, 'head', [(d, d ^ mask) for d in range(ways)])]
    all_to_all x1, starting transfers between devices: 4.4 us -> 24.7 us  [shards(): lax.all_to_all(local_attention, 'head', split_axis=0, concat_axis=1, tile...]
    unnamed x75 -> x73, local copies, waits for them, and re-layouts: 23.6 us -> 23.7 us
  transfers between devices with their start and end apart: 12 -> 14, of which waited for: 9 -> 10; matrix products, arithmetic and copies ran while one was open for 18% -> 19% of each run, Pallas kernels for 0% -> 0%
where the time goes in v1:
time: 1170 us; the launch traced here: 1150 us
  waiting for transfers between devices  546 us (47%)
  local copies, waits for them, and re-layouts  207 us (18%)
  blocking collectives  180 us (15%)
  matrix products  116 us (10%)
  other arithmetic  39.6 us (3%)
  starting transfers between devices  38.5 us (3%)
  between operations  14.9 us (1%)
  loops' own time  12 us (1%)
    reduce_scatter x1, waiting for transfers between devices, shards(): lax.psum_scatter(grad_up, ('seq', 'head'), scatter_dimension=1, tiled=True)  147 us
    reduce_scatter x1, waiting for transfers between devices, shards(): lax.psum_scatter(grad_qkv, ('seq', 'head'), scatter_dimension=0, tiled=True)  104 us
    reduce_scatter x1, waiting for transfers between devices, shards(): lax.psum_scatter(grad_down, ('seq', 'head'), scatter_dimension=0, tiled=T...  92.1 us
    all_gather x1, blocking collectives, shards(): lax.all_gather(w_out, ('seq', 'head'), axis=0, tiled=True)  90.7 us
    unnamed x2, blocking collectives  80.3 us
    all_to_all x1, waiting for transfers between devices, shards(): lax.all_to_all(d_qkv_local, 'head', split_axis=0, concat_axis=1, tiled=True)  76.9 us
    reduce_scatter x1, waiting for transfers between devices, shards(): lax.psum_scatter(grad_out, ('seq', 'head'), scatter_dimension=0, tiled=True)  46.2 us
    ppermute x3, waiting for transfers between devices, shards(): part = lax.ppermute(part, 'head', [(d, d ^ mask) for d in range(ways)])  44.7 us
  transfers between devices with their start and end apart: 14, of which 10 were waited for; matrix products, arithmetic and copies ran while one was open for 19% of the time, Pallas kernels for 0%

profile of v1, /device:TPU:0, one launch (start us, length us, event | category | flops | bytes accessed | tf_op | source)
XLA Modules:
  0.0 1154.7 jit_solution(8404542834195029461)
XLA Ops:
  12.1 42.1 %all-reduce.12 = (bf16[512]{0:T(512)(128)(2,1)S(1)}, bf16[512]{0:T(512)(128)(2,1)S(1)}, bf16[512]{0:T(512)(128)(2,1)}, bf16[512]{0:T(512)(128)(2,1)}) all-reduce(bf16[512]{0:T(512)(128)(2,1)S(1)} %dynamic-update-slice.7, bf16[512]{0:T(512)(128)(2,1)S(1)} %dynamic-update-slice.6, ...), channel_id=1, replica_groups=mesh['seq'=8,'head'=4] {'seq','head'}, use_global_device_ids=true, to_apply=%add.4 | all-reduce | flops 2048 | bytes 8192
  56.9 11.8 %all-gather.4.cloned.1.call-done = bf16[512,1536]{1,0:T(8,128)(2,1)} async-done(((bf16[16,1536]{1,0:T(8,128)(2,1)}), bf16[512,1536]{1,0:T(8,128)(2,1)}) %all-gather.4.cloned.1.call-update) | async-done | bytes 1572880 | tf_op jit(solution)/shard_map/all_gather | solution.py:87
  68.7 3.4 convolution_convert_fusion
  81.4 32.1 %collective-permute-done.1 = bf16[1024,384]{1,0:T(8,128)(2,1)} collective-permute-done((bf16[1024,384]{1,0:T(8,128)(2,1)}, bf16[1024,384]{1,0:T(8,128)(2,1)}, u32[]{:S(2)}, u32[]{:S(2)}) %collective-permute-start.1) | collective-permute-done | bytes 786464 | tf_op jit(solution)/shard_map/ppermute | solution.py:117
  118.3 12.7 %collective-permute-done.2 = bf16[1024,384]{1,0:T(8,128)(2,1)S(1)} collective-permute-done((bf16[1024,384]{1,0:T(8,128)(2,1)}, bf16[1024,384]{1,0:T(8,128)(2,1)S(1)}, u32[]{:S(2)}, u32[]{:S(2)}) %collective-permute-start.2) | collective-permute-done | bytes 786464 | tf_op jit(solution)/shard_map/ppermute | solution.py:117
  132.2 3.5 fusion.89
  135.7 4.0 slice_convert_fusion
  140.9 2.7 reshape_squeeze.9
  146.8 4.9 copy.241
  151.8 3.4 reduce_sum.178
  155.2 9.3 all_gather.30
  165.9 68.9 %while.33 = (s32[]{:T(128)}, bf16[8,512,128]{2,1,0:T(8,128)(2,1)}, f32[8,2,4,128]{3,2,1,0:T(4,128)}, bf16[8,4,128,2,64]{2,1,0,4,3:T(4,128)(2,1)}, bf16[8,4,128,2...) while((s32[]{:T(128)}, bf16[8,512,128]{2,1,0:T(8,128)(2,1)}, ...), condition=%wide.region_8.9_spmd, body=%wide.region_3.8_spmd.sunk | while | flops 74914296 | bytes 5989179 | solution.py:159
  234.8 24.7 %all-to-all-start = ((bf16[4,1024,128]{2,1,0:T(8,128)(2,1)}), bf16[4,1024,128]{2,1,0:T(8,128)(2,1)}, u32[]{:S(2)}, u32[]{:S(2)}) async-start(bf16[4,1024,128]{2,1,0:T(8,128)(2,1)} %bitcast.293), calls=%async_computation | async-start | bytes 2097152 | tf_op jit(solution)/shard_map/all_to_all | solution.py:161
  260.2 2.3 copy.182
  262.4 90.7 %all_gather.31 = bf16[512,512]{1,0:T(8,128)(2,1)} all-gather(bf16[16,512]{1,0:T(8,128)(2,1)S(1)} %copy-done.17), channel_id=1, replica_groups=mesh['seq'=8,'head'=4] {'seq','head'}, dimensions={0}, use_global_device_ids=true | all-gather | bytes 540672 | tf_op jit(solution)/shard_map/all_gather | solution.py:88
  358.2 7.6 fusion.83
  365.7 9.7 fusion.63
  375.4 3.6 fusion.92
  379.1 2.9 copy.183
  382.0 2.4 multiply_reduce_fusion.2
  388.4 3.5 all-to-all-start.1
  392.2 20.8 %all-to-all-done.1 = bf16[1024,4,128]{0,2,1:T(8,128)(2,1)S(1)} async-done(((bf16[1024,4,128]{0,2,1:T(8,128)(2,1)}), bf16[1024,4,128]{0,2,1:T(8,128)(2,1)S(1)}, u32[]{:S(2)}, u32[]{:S(2)}) %all-to-all-start.1) | async-done | bytes 1048608 | tf_op jit(solution)/shard_map/all_to_all | solution.py:180
  417.0 120.3 %while.34 = (s32[]{:T(128)}, f32[256,2,2,64]{0,3,1,2:T(8,128)S(1)}, bf16[8,4,128,2,64]{2,4,3,1,0:T(8,128)(2,1)}, f32[8,4,128,2,64]{2,1,0,4,3:T(4,128)}, f32[8,4,...) while((s32[]{:T(128)}, f32[256,2,2,64]{0,3,1,2:T(8,128)S(1)}, ...), condition=%wide.region_16.17_spmd, body=%wide.region_13.16_spmd.sunk | while | flops 183960576 | bytes 14116731 | solution.py:234
  538.2 3.3 fusion.93
  541.6 9.1 fusion.84
  552.3 6.7 fusion.82
  559.0 3.1 reshape.339
  562.1 3.0 copy.189
  565.1 2.7 stack_reshape.6
  567.7 3.0 reshape.338
  574.3 2.7 add.347
  579.0 2.7 add.351
  581.8 4.1 add_convert_fusion
  588.2 6.2 convert_element_type.128
  594.4 4.6 copy.194
  599.0 4.8 all-to-all-start.2
  604.0 76.9 %all-to-all-done.2 = bf16[4,1024,384]{1,2,0:T(8,128)(2,1)} async-done(((bf16[4,1024,384]{1,2,0:T(8,128)(2,1)}), bf16[4,1024,384]{1,2,0:T(8,128)(2,1)}, u32[]{:S(2)}, u32[]{:S(2)}) %all-to-all-start.2) | async-done | bytes 3145760 | tf_op jit(solution)/shard_map/all_to_all | solution.py:255
  680.9 5.6 fusion.79
  686.5 8.4 add_convert_fusion.2
  694.9 2.4 copy.198
  697.3 46.2 %reduce-scatter.10.cloned.1.call-done = f32[16,512]{1,0:T(8,128)} async-done(((f32[512,512]{1,0:T(8,128)}), f32[16,512]{1,0:T(8,128)}) %reduce-scatter.10.cloned.1.call-update) | async-done | bytes 32784 | tf_op jit(solution)/shard_map/reduce_scatter | solution.py:271
  744.8 5.1 fusion.91
  754.4 2.3 add_add_fusion.2
  756.6 2.9 copy.199
  759.5 38.1 %all-reduce.11 = (f32[512]{0:T(512)S(1)}, f32[512]{0:T(512)S(1)}, f32[512]{0:T(512)S(1)}, f32[512]{0:T(512)S(1)}) all-reduce(f32[512]{0:T(512)S(1)} %get-tuple-element.526, f32[512]{0:T(512)S(1)} %get-tuple-element.621, f32[512]{0:T(512)S(1)} %get-tuple-element.524, ...), channel_id=7, replica_groups=mesh['seq'=8,'head'=4] {'seq','head'}, use_global_device_ids=true, to_apply=%region_25.26.clone | all-reduce | flops 2048 | bytes 16384
  800.0 92.1 %reduce-scatter.14.cloned.1.call-done = f32[64,512]{1,0:T(8,128)} async-done(((f32[2048,512]{1,0:T(8,128)}), f32[64,512]{1,0:T(8,128)}) %reduce-scatter.14.cloned.1.call-update) | async-done | bytes 131088 | tf_op jit(solution)/shard_map/reduce_scatter | solution.py:273
  893.7 146.6 %reduce-scatter.12.cloned.1.call-done = f32[512,64]{0,1:T(8,128)} async-done(((f32[512,2048]{0,1:T(8,128)}), f32[512,64]{0,1:T(8,128)}) %reduce-scatter.12.cloned.1.call-update) | async-done | bytes 131088 | tf_op jit(solution)/shard_map/reduce_scatter | solution.py:272
  1041.8 104.3 %reduce-scatter.8.cloned.1.call-done = f32[16,1536]{1,0:T(8,128)} async-done(((f32[512,1536]{1,0:T(8,128)}), f32[16,1536]{1,0:T(8,128)}) %reduce-scatter.8.cloned.1.call-update) | async-done | bytes 98320 | tf_op jit(solution)/shard_map/reduce_scatter | solution.py:270
  (656 shorter events, 242.9 us)
Async XLA Ops:
  7.2 61.5 %all-gather.4.cloned.1.call-start = ((), (), s32[]{:S(2)}) async-start(), calls=%async_computation.8 | async-start | bytes 1622016 | tf_op jit(solution)/shard_map/all_gather | solution.py:87
  7.9 349.9 %all-gather.6.cloned.1.call-start = ((), (), s32[]{:S(2)}) async-start(), calls=%async_computation.9 | async-start | bytes 2162688 | tf_op jit(solution)/shard_map/all_gather | solution.py:89
  8.7 357.1 %all-gather.8.cloned.1.call-start = ((), (), s32[]{:S(2)}) async-start(), calls=%async_computation.10 | async-start | bytes 2162688 | tf_op jit(solution)/shard_map/all_gather | solution.py:90
  54.3 14.4 %copy-start.18 = (f32[512]{0:T(512)}, f32[512]{0:T(512)S(1)}, u32[]{:S(2)}) copy-start(f32[512]{0:T(512)S(1)} %convert_element_type.110) | copy-start | bytes 6148
  56.3 0.6 copy-start.15
  72.1 6.0 copy-start.25
  73.6 39.9 %collective-permute-start.1 = (bf16[1024,384]{1,0:T(8,128)(2,1)}, bf16[1024,384]{1,0:T(8,128)(2,1)}, u32[]{:S(2)}, u32[]{:S(2)}) collective-permute-start(bf16[1024,384]{1,0:T(8,128)(2,1)} %get-tuple-element.612), channel_id=1, source_target_pairs={{0,2},{1,3},{2,0},{3,1},{4,6},{5,7},{6,4},{7,5},{8,10},{9,11},{10,... | collective-permute-start | bytes 2359304 | tf_op jit(solution)/shard_map/ppermute | solution.py:117
  74.4 40.5 %collective-permute-start = (bf16[1024,384]{1,0:T(8,128)(2,1)}, bf16[1024,384]{1,0:T(8,128)(2,1)}, u32[]{:S(2)}, u32[]{:S(2)}) collective-permute-start(bf16[1024,384]{1,0:T(8,128)(2,1)} %get-tuple-element.613), channel_id=1, source_target_pairs={{0,1},{1,0},{2,3},{3,2},{4,5},{5,4},{6,7},{7,6},{8,9},{9,8},{10,11... | collective-permute-start | bytes 2359304 | tf_op jit(solution)/shard_map/ppermute | solution.py:117
  76.4 54.5 %collective-permute-start.2 = (bf16[1024,384]{1,0:T(8,128)(2,1)}, bf16[1024,384]{1,0:T(8,128)(2,1)S(1)}, u32[]{:S(2)}, u32[]{:S(2)}) collective-permute-start(bf16[1024,384]{1,0:T(8,128)(2,1)} %get-tuple-element.611), channel_id=1, source_target_pairs={{0,3},{1,2},{2,1},{3,0},{4,7},{5,6},{6,5},{7,4},{8,11},{9,10},{10,... | collective-permute-start | bytes 2359304 | tf_op jit(solution)/shard_map/ppermute | solution.py:117
  140.9 2.7 copy-start.11
  234.8 24.8 %copy-start.23 = (s32[256]{0:T(256)}, s32[256]{0:T(256)S(1)}, u32[]{:S(2)}) copy-start(s32[256]{0:T(256)S(1)} %get-tuple-element.973) | copy-start | bytes 3076
  234.8 27.6 %copy-start.2 = (bf16[8,4,128,2,64]{2,4,1,3,0:T(8,128)(2,1)}, bf16[8,4,128,2,64]{2,4,1,3,0:T(8,128)(2,1)S(1)}, u32[]{:S(2)}) copy-start(bf16[8,4,128,2,64]{2,4,1,3,0:T(8,128)(2,1)S(1)} %get-tuple-element.943) | copy-start | bytes 3145732
  234.8 27.6 %copy-start.9 = (bf16[8,4,128,2,64]{2,4,1,3,0:T(8,128)(2,1)}, bf16[8,4,128,2,64]{2,4,1,3,0:T(8,128)(2,1)S(1)}, u32[]{:S(2)}) copy-start(bf16[8,4,128,2,64]{2,4,1,3,0:T(8,128)(2,1)S(1)} %get-tuple-element.946) | copy-start | bytes 3145732
  234.8 24.8 %copy-start.22 = (bf16[512]{0:T(512)(128)(2,1)S(1)}, bf16[512]{0:T(512)(128)(2,1)}, u32[]{:S(2)}) copy-start(bf16[512]{0:T(512)(128)(2,1)} %get-tuple-element.587) | copy-start | bytes 3076
  234.8 24.8 %copy-start.21 = (bf16[512]{0:T(512)(128)(2,1)S(1)}, bf16[512]{0:T(512)(128)(2,1)}, u32[]{:S(2)}) copy-start(bf16[512]{0:T(512)(128)(2,1)} %get-tuple-element.586) | copy-start | bytes 3076
  234.8 27.6 %copy-start.17 = (bf16[16,512]{1,0:T(8,128)(2,1)S(1)}, bf16[16,512]{1,0:T(8,128)(2,1)}, u32[]{:S(2)}) copy-start(bf16[16,512]{1,0:T(8,128)(2,1)} %param.20) | copy-start | bytes 49156
  234.8 118.3 %all-to-all-start = ((bf16[4,1024,128]{2,1,0:T(8,128)(2,1)}), bf16[4,1024,128]{2,1,0:T(8,128)(2,1)}, u32[]{:S(2)}, u32[]{:S(2)}) async-start(bf16[4,1024,128]{2,1,0:T(8,128)(2,1)} %bitcast.293), calls=%async_computation | async-start | bytes 2097152 | tf_op jit(solution)/shard_map/all_to_all | solution.py:161
  357.5 26.9 %copy-start = (f32[1024,512]{0,1:T(8,128)}, f32[1024,512]{0,1:T(8,128)S(1)}, u32[]{:S(2)}) copy-start(f32[1024,512]{0,1:T(8,128)S(1)} %get-tuple-element.620) | copy-start | bytes 6291460
  357.5 0.7 copy-start.20
  365.7 9.7 copy-start.26
  375.4 3.7 copy-start.28
  382.0 2.4 copy-start.4
  384.4 1.2 copy-start.7
  384.9 1.3 copy-start.5
  385.6 1.1 copy-start.12
  386.7 1.7 copy-start.13
  388.4 24.6 %all-to-all-start.1 = ((bf16[1024,4,128]{0,2,1:T(8,128)(2,1)}), bf16[1024,4,128]{0,2,1:T(8,128)(2,1)S(1)}, u32[]{:S(2)}, u32[]{:S(2)}) async-start(bf16[1024,4,128]{0,2,1:T(8,128)(2,1)} %bitcast.42), calls=%async_computation.1 | async-start | bytes 2097152 | tf_op jit(solution)/shard_map/all_to_all | solution.py:180
  391.9 179.6 %reduce-scatter.16.cloned.1.call-start = ((), (), s32[]{:S(2)}) async-start(), calls=%async_computation.15 | async-start | bytes 147456
  413.0 4.0 copy-start.3
  413.0 4.1 copy-start.24
  538.1 3.5 copy-start.14
  538.2 205.3 %reduce-scatter.10.cloned.1.call-start = ((), (), s32[]{:S(2)}) async-start(), calls=%async_computation.12 | async-start | bytes 1081344 | tf_op jit(solution)/shard_map/reduce_scatter | solution.py:271
  541.6 350.5 %reduce-scatter.14.cloned.1.call-start = ((), (), s32[]{:S(2)}) async-start(), calls=%async_computation.14 | async-start | bytes 4325376 | tf_op jit(solution)/shard_map/reduce_scatter | solution.py:273
  550.7 1.6 copy-start.1
  550.7 489.5 %reduce-scatter.12.cloned.1.call-start = ((), (), s32[]{:S(2)}) async-start(), calls=%async_computation.13 | async-start | bytes 4325376 | tf_op jit(solution)/shard_map/reduce_scatter | solution.py:272
  581.8 4.1 copy-start.10
  599.0 81.9 %copy-start.19 = (f32[512]{0:T(512)S(1)}, f32[512]{0:T(512)}, u32[]{:S(2)}) copy-start(f32[512]{0:T(512)} %copy-done.18) | copy-start | bytes 6148
  599.0 81.9 %all-to-all-start.2 = ((bf16[4,1024,384]{1,2,0:T(8,128)(2,1)}), bf16[4,1024,384]{1,2,0:T(8,128)(2,1)}, u32[]{:S(2)}, u32[]{:S(2)}) async-start(bf16[4,1024,384]{1,2,0:T(8,128)(2,1)} %copy.194), calls=%async_computation.2 | async-start | bytes 6291456 | tf_op jit(solution)/shard_map/all_to_all | solution.py:255
  603.8 542.3 %reduce-scatter.8.cloned.1.call-start = ((), (), s32[]{:S(2)}) async-start(), calls=%async_computation.11 | async-start | bytes 3244032 | tf_op jit(solution)/shard_map/reduce_scatter | solution.py:270
  694.9 50.0 %copy-start.27 = (bf16[512,1536]{1,0:T(8,128)(2,1)S(1)}, bf16[512,1536]{1,0:T(8,128)(2,1)}, u32[]{:S(2)}) copy-start(bf16[512,1536]{1,0:T(8,128)(2,1)} %all-gather.4.cloned.1.call-done) | copy-start | bytes 4718596
  751.8 0.7 copy-start.16
  752.5 1.6 copy-start.6
  752.5 1.9 copy-start.8
Sparse Core Ops, SparseCore 0:
  10.9 57.7 all-gather.3
  71.6 86.4 all-gather.5
  161.1 55.4 all-gather.7
  538.3 33.2 reduce-scatter.15
  573.7 169.7 reduce-scatter.9
  745.6 146.4 reduce-scatter.13
  894.4 145.8 reduce-scatter.11
  1045.7 100.4 reduce-scatter.7
